TPU v7x, 32 devices: a whole 2x2x4 slice. The times are simulated.
32 devices in a mesh: fsdp: 4 (over x, core), tok: 8 (over z, y).
Axes of the slice: x: 2, y: 2, z: 4, core: 2. Of those that a mesh axis runs over, the one named last changes fastest.
Arguments:
- states: bfloat16 [4, 512, 1024], P('fsdp', 'tok'), may hold values from -8 to 8
- cache_keys: bfloat16 [4, 1024, 1024], P('fsdp', 'tok'), may hold values from -6 to 6
- cache_values: bfloat16 [4, 1024, 1024], P('fsdp', 'tok'), may hold values from -6 to 6
- cache_len: int32 [4], P('fsdp'), may hold values from 1 to 1024, as said below
- token_slot: int32 [4, 512], P('fsdp', 'tok'), may hold values from 0 to 511, as said below
- bucket_table: int32 [1536], replicated, may hold values from 0 to 31
- rel_bias: float32 [32, 16], replicated, may hold values from -3 to 250
- norm_gain: float32 [1024], replicated, may hold values from 0.5 to 1.5
- w_query: bfloat16 [1024, 1024], P(('fsdp', 'tok')), may hold values from -0.0234375 to 0.0234375
- w_key: bfloat16 [1024, 1024], P(('fsdp', 'tok')), may hold values from -0.1875 to 0.1875
- w_value: bfloat16 [1024, 1024], P(('fsdp', 'tok')), may hold values from -0.1875 to 0.1875
- w_out: bfloat16 [1024, 1024], P(('fsdp', 'tok')), may hold values from -1.5 to 1.5
Outputs:
- hidden_out: bfloat16 [4, 512, 1024], P('fsdp', 'tok')
- new_keys: bfloat16 [4, 512, 1024], P('fsdp', 'tok')
- new_values: bfloat16 [4, 512, 1024], P('fsdp', 'tok')
Inputs may be any that keep to these rules, and one draw needn't show every extreme that they name: `cache_len`: one request has exactly 1024 live rows. `token_slot`: each row is a permutation of 0 to 511; every aligned block of 64 tokens of a request has exactly 8 of its slots in each aligned block of 64 slots.
All inputs are finite; a program needn't handle non-finite values.
Results may differ from a plain program's by a relative error of at most 0.0095.
Values may be sent and summed in bfloat16 or wider, within the bound.
No kernel may reach another device: no remote copies, remote signals or barrier semaphores. Data moves between devices by JAX's collectives and lax.ppermute only.
A program may use at most 64 MiB of HBM per device.

v0:
```python
import jax
import jax.numpy as jnp
from jax import lax
from jax.sharding import PartitionSpec as P

far_away = 1073741824
neg_floor = -1e30


def bias_scores(bucket_ids, bias_parts):
    bucket_count = bias_parts[0].shape[0]
    one_hot = (bucket_ids[..., None] == jnp.arange(bucket_count, dtype=jnp.int32)).astype(
        jnp.bfloat16
    )
    high_part = jnp.einsum(
        "qkb,bh->hqk", one_hot, bias_parts[0], preferred_element_type=jnp.float32
    )
    middle = jnp.einsum("qkb,bh->hqk", one_hot, bias_parts[1], preferred_element_type=jnp.float32)
    low_part = jnp.einsum("qkb,bh->hqk", one_hot, bias_parts[2], preferred_element_type=jnp.float32)
    return high_part + middle + low_part


def absorb(running, queries, query_pos, keys_here, values_here, key_pos, bucket_table, bias_parts):
    totals, peak_old, masses = running
    head_count = queries.shape[1]
    keys_split = keys_here.reshape(keys_here.shape[0], head_count, -1)
    values_split = values_here.reshape(values_here.shape[0], head_count, -1)
    scores = jnp.einsum("qhd,khd->hqk", queries, keys_split, preferred_element_type=jnp.float32)
    distance = query_pos[:, None] - key_pos[None, :]
    allowed = (distance >= 0)[None]
    bucket_ids = jnp.take(bucket_table, jnp.clip(distance, 0, bucket_table.shape[0] - 1), axis=0)
    scores = scores + bias_scores(bucket_ids, bias_parts)
    new_peak = jnp.maximum(peak_old, jnp.max(jnp.where(allowed, scores, neg_floor), axis=-1))
    weights = jnp.where(allowed, jnp.exp(scores - new_peak[..., None]), 0.0)
    shrink = jnp.exp(peak_old - new_peak)
    masses = masses * shrink + jnp.sum(weights, axis=-1)
    totals = totals * jnp.transpose(shrink)[..., None] + jnp.einsum(
        "hqk,khd->qhd",
        weights.astype(jnp.bfloat16),
        values_split,
        preferred_element_type=jnp.float32,
    )
    return (totals, new_peak, masses)


def permute_rows(selector, rows):
    return jnp.dot(selector.astype(jnp.bfloat16), rows, preferred_element_type=jnp.float32).astype(
        jnp.bfloat16
    )


def permute_ints(selector, values):
    return jnp.sum(jnp.where(selector, values[None, :], 0), axis=1).astype(jnp.int32)


def shards(
    states,
    cache_keys,
    cache_values,
    cache_len,
    token_slot,
    bucket_table,
    rel_bias,
    norm_gain,
    w_query,
    w_key,
    w_value,
    w_out,
):
    peer_count = lax.axis_size("tok")
    my_index = lax.axis_index("tok")
    tokens = states[0]
    tok_rows = tokens.shape[0]
    feature_count = tokens.shape[1]
    per_peer = tok_rows // peer_count
    head_count = rel_bias.shape[1]
    head_size = feature_count // head_count
    slot_ids = token_slot[0]
    length = cache_len[0]
    row_iota = jnp.arange(tok_rows, dtype=jnp.int32)
    ranking = jnp.sum((slot_ids[None, :] < slot_ids[:, None]).astype(jnp.int32), axis=1)
    sort_sel = ranking[None, :] == row_iota[:, None]
    sent_rows = permute_rows(sort_sel, tokens).reshape(peer_count, per_peer, feature_count)
    sent_slots = permute_ints(sort_sel, slot_ids).reshape(peer_count, per_peer)
    sent_pos = (my_index * tok_rows + permute_ints(sort_sel, row_iota)).reshape(
        peer_count, per_peer
    )
    got_rows, got_slots, got_pos = (
        lax.all_to_all(sent_rows, "tok", split_axis=0, concat_axis=0, tiled=True),
        lax.all_to_all(sent_slots, "tok", split_axis=0, concat_axis=0, tiled=True),
        lax.all_to_all(sent_pos, "tok", split_axis=0, concat_axis=0, tiled=True),
    )
    local_slot = got_slots.reshape(tok_rows) - my_index * tok_rows
    place_sel = local_slot[None, :] == row_iota[:, None]
    dealt = permute_rows(place_sel, got_rows.reshape(tok_rows, feature_count))
    dealt_pos = permute_ints(place_sel, got_pos.reshape(tok_rows))
    query_w, key_w, value_w, out_w = (
        lax.all_gather(w_query, ("fsdp", "tok"), axis=0, tiled=True),
        lax.all_gather(w_key, ("fsdp", "tok"), axis=0, tiled=True),
        lax.all_gather(w_value, ("fsdp", "tok"), axis=0, tiled=True),
        lax.all_gather(w_out, ("fsdp", "tok"), axis=0, tiled=True),
    )
    wide_in = dealt.astype(jnp.float32)
    inverse = lax.rsqrt(jnp.mean(wide_in * wide_in, axis=-1, keepdims=True) + 1e-06)
    normed = (wide_in * inverse * norm_gain).astype(jnp.bfloat16)
    queries = jnp.dot(normed, query_w, preferred_element_type=jnp.float32).astype(jnp.bfloat16)
    new_keys = jnp.dot(normed, key_w, preferred_element_type=jnp.float32).astype(jnp.bfloat16)
    new_values = jnp.dot(normed, value_w, preferred_element_type=jnp.float32).astype(jnp.bfloat16)
    query_pos = length + dealt_pos
    cache_rows = cache_keys.shape[1]
    cache_spot = my_index * cache_rows + jnp.arange(cache_rows, dtype=jnp.int32)
    key_pos = jnp.concatenate([jnp.where(cache_spot < length, cache_spot, far_away), query_pos])
    keys_here = jnp.concatenate([cache_keys[0], new_keys])
    values_here = jnp.concatenate([cache_values[0], new_values])
    bias_high = rel_bias.astype(jnp.bfloat16)
    remainder = rel_bias - bias_high.astype(jnp.float32)
    bias_middle = remainder.astype(jnp.bfloat16)
    bias_low = (remainder - bias_middle.astype(jnp.float32)).astype(jnp.bfloat16)
    bias_parts = (bias_high, bias_middle, bias_low)
    query_heads = queries.reshape(tok_rows, head_count, head_size)
    shard_len = keys_here.shape[0]
    initial = (
        jnp.zeros((tok_rows, head_count, head_size), jnp.float32),
        jnp.full((head_count, tok_rows), neg_floor, jnp.float32),
        jnp.zeros((head_count, tok_rows), jnp.float32),
    )
    running = initial
    part_keys = lax.all_gather(keys_here, "tok", axis=0, tiled=True)
    part_values = lax.all_gather(values_here, "tok", axis=0, tiled=True)
    part_pos = lax.all_gather(key_pos, "tok", axis=0, tiled=True)
    rows_in = part_keys.shape[0]
    block_len = 2 * shard_len
    shard_count = rows_in // block_len
    blocks = (
        part_keys.reshape(shard_count, block_len, feature_count),
        part_values.reshape(shard_count, block_len, feature_count),
        part_pos.reshape(shard_count, block_len),
    )

    def advance(running_in, block_set):
        return (
            absorb(
                running_in,
                query_heads,
                query_pos,
                block_set[0],
                block_set[1],
                block_set[2],
                bucket_table,
                bias_parts,
            ),
            None,
        )

    running, unused = lax.scan(advance, running, blocks)
    totals, peaks, masses = running
    context = (
        (totals / jnp.transpose(masses)[..., None])
        .reshape(tok_rows, feature_count)
        .astype(jnp.bfloat16)
    )
    result_dealt = (wide_in + jnp.dot(context, out_w, preferred_element_type=jnp.float32)).astype(
        jnp.bfloat16
    )
    back_rows = permute_rows(jnp.transpose(place_sel), result_dealt).reshape(
        peer_count, per_peer, feature_count
    )
    returned = lax.all_to_all(back_rows, "tok", split_axis=0, concat_axis=0, tiled=True)
    hidden = permute_rows(jnp.transpose(sort_sel), returned.reshape(tok_rows, feature_count))
    return (hidden[None], new_keys[None], new_values[None])


def solution(mesh):
    in_specs = (
        P("fsdp", "tok", None),
        P("fsdp", "tok", None),
        P("fsdp", "tok", None),
        P("fsdp"),
        P("fsdp", "tok"),
        P(),
        P(),
        P(),
        P(("fsdp", "tok"), None),
        P(("fsdp", "tok"), None),
        P(("fsdp", "tok"), None),
        P(("fsdp", "tok"), None),
    )
    out_specs = (P("fsdp", "tok", None), P("fsdp", "tok", None), P("fsdp", "tok", None))
    return jax.shard_map(shards, mesh=mesh, in_specs=in_specs, out_specs=out_specs, check_vma=False)
```

profile of v0, /device:TPU:0, one launch (start us, length us, event | category | flops | bytes accessed | tf_op | source)
XLA Modules:
  0.0 936.9 jit_solution(472488924100509051)
XLA Ops:
  11.8 7.3 all-to-all-start
  19.9 5.6 all-to-all-done
  25.4 3.4 all-to-all-start.1
  29.0 7.2 all-to-all-done.1
  38.0 32.8 %all-gather.13.cloned.1.call-done = bf16[1024,1024]{1,0:T(8,128)(2,1)} async-done(((bf16[32,1024]{1,0:T(8,128)(2,1)}), bf16[1024,1024]{1,0:T(8,128)(2,1)}) %all-gather.13.cloned.1.call-update) | async-done | bytes 2097168 | tf_op jit(solution)/shard_map/all_gather | solution.py:100
  74.4 54.8 %all-gather.7.cloned.1.call-done = bf16[1024,1024]{1,0:T(8,128)(2,1)} async-done(((bf16[32,1024]{1,0:T(8,128)(2,1)}), bf16[1024,1024]{1,0:T(8,128)(2,1)}) %all-gather.7.cloned.1.call-update) | async-done | bytes 2097168 | tf_op jit(solution)/shard_map/all_gather | solution.py:99
  133.4 4.4 all-to-all-start.2
  140.4 3.7 all-to-all-done.2
  145.7 8.7 all-reduce
  154.4 33.1 %all-gather.11.cloned.1.call-done = bf16[1024,1024]{1,0:T(8,128)(2,1)} async-done(((bf16[32,1024]{1,0:T(8,128)(2,1)}), bf16[1024,1024]{1,0:T(8,128)(2,1)}) %all-gather.11.cloned.1.call-update) | async-done | bytes 2097168 | tf_op jit(solution)/shard_map/all_gather | solution.py:98
  190.6 58.3 %all-gather.15.cloned.1.call-done = bf16[1536,1024]{1,0:T(8,128)(2,1)} async-done(((bf16[192,1024]{1,0:T(8,128)(2,1)}), bf16[1536,1024]{1,0:T(8,128)(2,1)}) %all-gather.15.cloned.1.call-update) | async-done | bytes 3145744 | tf_op jit(solution)/shard_map/all_gather | solution.py:129
  249.0 61.1 %all-gather.9.cloned.1.call-done = bf16[1536,1024]{1,0:T(8,128)(2,1)} async-done(((bf16[192,1024]{1,0:T(8,128)(2,1)}), bf16[1536,1024]{1,0:T(8,128)(2,1)}) %all-gather.9.cloned.1.call-update) | async-done | bytes 3145744 | tf_op jit(solution)/shard_map/all_gather | solution.py:128
  310.1 605.3 %while.15 = (s32[]{:T(128)}, f32[64,16,64]{0,2,1:T(8,128)}, f32[16,64]{1,0:T(8,128)S(1)}, f32[16,64]{1,0:T(8,128)S(1)}, s32[64]{0:T(128)S(1)}, /*index=5*/s32[4,...) while((s32[]{:T(128)}, f32[64,16,64]{0,2,1:T(8,128)}, ...), condition=%wide.region_8.9_spmd.clone, body=%wide.region_5.8_spmd.clone.sunk | while | flops 183465984 | bytes 27471288 | solution.py:155
  310.3 135.5 %gather_fusion = s32[24576]{0:T(1024)S(1)} fusion(s32[1536]{0:T(1024)S(1)} %get-tuple-element.335, s32[24576]{0:T(1024)S(1)} %broadcast_clamp_fusion.2), kind=kCustom, calls=%fused_computation.clone.clone.1 | custom fusion | bytes 294912 | tf_op jit(solution)/shard_map/while/body/eval_jaxpr/jit(_take)/gather | solution.py:31
  453.7 4.1 select_reduce_fusion.5
  460.8 135.5 %gather_fusion = s32[24576]{0:T(1024)S(1)} fusion(s32[1536]{0:T(1024)S(1)} %get-tuple-element.335, s32[24576]{0:T(1024)S(1)} %broadcast_clamp_fusion.2), kind=kCustom, calls=%fused_computation.clone.clone.1 | custom fusion | bytes 294912 | tf_op jit(solution)/shard_map/while/body/eval_jaxpr/jit(_take)/gather | solution.py:31
  604.2 4.1 select_reduce_fusion.5
  609.8 2.4 fusion.74
  612.4 135.5 %gather_fusion = s32[24576]{0:T(1024)S(1)} fusion(s32[1536]{0:T(1024)S(1)} %get-tuple-element.335, s32[24576]{0:T(1024)S(1)} %broadcast_clamp_fusion.2), kind=kCustom, calls=%fused_computation.clone.clone.1 | custom fusion | bytes 294912 | tf_op jit(solution)/shard_map/while/body/eval_jaxpr/jit(_take)/gather | solution.py:31
  755.8 4.1 select_reduce_fusion.5
  761.4 2.4 fusion.74
  764.0 135.5 %gather_fusion = s32[24576]{0:T(1024)S(1)} fusion(s32[1536]{0:T(1024)S(1)} %get-tuple-element.335, s32[24576]{0:T(1024)S(1)} %broadcast_clamp_fusion.2), kind=kCustom, calls=%fused_computation.clone.clone.1 | custom fusion | bytes 294912 | tf_op jit(solution)/shard_map/while/body/eval_jaxpr/jit(_take)/gather | solution.py:31
  907.4 4.1 select_reduce_fusion.5
  918.8 10.4 %all_to_all.25 = bf16[8,8,1024]{2,1,0:T(8,128)(2,1)S(1)} all-to-all(bf16[8,8,1024]{2,1,0:T(8,128)(2,1)S(1)} %fusion.25), channel_id=1, replica_groups=mesh['fsdp'=4,'tok'=8] {'tok'}, dimensions={0} | all-to-all | bytes 262144 | tf_op jit(solution)/shard_map/all_to_all | solution.py:168
  (152 shorter events, 66.7 us)
Async XLA Ops:
  7.2 11.9 %copy-start = (bf16[1,64,1024]{2,1,0:T(8,128)(2,1)S(1)}, bf16[1,64,1024]{2,1,0:T(8,128)(2,1)}, u32[]{:S(2)}) copy-start(bf16[1,64,1024]{2,1,0:T(8,128)(2,1)} %param.14) | copy-start | bytes 393220
  7.2 63.6 %all-gather.13.cloned.1.call-start = ((), (), s32[]{:S(2)}) async-start(), calls=%async_computation.7 | async-start | bytes 2162688 | tf_op jit(solution)/shard_map/all_gather | solution.py:100
  7.9 121.3 %all-gather.7.cloned.1.call-start = ((), (), s32[]{:S(2)}) async-start(), calls=%async_computation.4 | async-start | bytes 2162688 | tf_op jit(solution)/shard_map/all_gather | solution.py:99
  8.7 178.9 %all-gather.11.cloned.1.call-start = ((), (), s32[]{:S(2)}) async-start(), calls=%async_computation.6 | async-start | bytes 2162688 | tf_op jit(solution)/shard_map/all_gather | solution.py:98
  10.3 15.1 %copy-start.11 = (s32[64]{0:T(128)}, s32[64]{0:T(128)S(1)}, u32[]{:S(2)}) copy-start(s32[64]{0:T(128)S(1)} %convert_reduce_fusion) | copy-start | bytes 772
  11.8 13.7 %all-to-all-start = ((s32[8,1,8]{2,1,0:T(1,128)}), s32[8,1,8]{2,1,0:T(1,128)S(1)}, u32[]{:S(2)}, u32[]{:S(2)}) async-start(s32[8,1,8]{2,1,0:T(1,128)} %bitcast.1), calls=%async_computation | async-start | bytes 8192 | tf_op jit(solution)/shard_map/all_to_all | solution.py:90
  25.4 10.8 %all-to-all-start.1 = ((bf16[8,8,1024]{2,1,0:T(8,128)(2,1)}), bf16[8,8,1024]{2,1,0:T(8,128)(2,1)S(1)}, u32[]{:S(2)}, u32[]{:S(2)}) async-start(bf16[8,8,1024]{2,1,0:T(8,128)(2,1)} %fusion.26), calls=%async_computation.1 | async-start | bytes 262144 | tf_op jit(solution)/shard_map/all_to_all | solution.py:89
  28.8 220.1 %all-gather.15.cloned.1.call-start = ((), (), s32[]{:S(2)}) async-start(), calls=%async_computation.8 | async-start | bytes 3538944 | tf_op jit(solution)/shard_map/all_gather | solution.py:129
  29.0 116.4 %copy-start.9 = (s32[64]{0:T(128)}, s32[64]{0:T(128)S(1)}, u32[]{:S(2)}) copy-start(s32[64]{0:T(128)S(1)} %sub.69) | copy-start | bytes 772
  29.0 44.5 %copy-start.6 = (bf16[1,128,1024]{2,1,0:T(8,128)(2,1)S(1)}, bf16[1,128,1024]{2,1,0:T(8,128)(2,1)}, u32[]{:S(2)}) copy-start(bf16[1,128,1024]{2,1,0:T(8,128)(2,1)} %param.16) | copy-start | bytes 786436
  36.5 0.7 copy-start.3
  74.3 57.6 %copy-start.7 = (bf16[1,128,1024]{2,1,0:T(8,128)(2,1)S(1)}, bf16[1,128,1024]{2,1,0:T(8,128)(2,1)}, u32[]{:S(2)}) copy-start(bf16[1,128,1024]{2,1,0:T(8,128)(2,1)} %param.15) | copy-start | bytes 786436
  74.3 64.7 %copy-start.8 = (f32[32,16]{0,1:T(8,128)S(1)}, f32[32,16]{0,1:T(8,128)}, u32[]{:S(2)}) copy-start(f32[32,16]{0,1:T(8,128)} %param.20) | copy-start | bytes 6148
  74.3 64.7 %copy-start.13 = (u32[32]{0:T(128)S(1)}, u32[32]{0:T(128)}, u32[]{:S(2)}) copy-start(u32[32]{0:T(128)} %constant.64) | copy-start | bytes 388
  74.4 235.7 %all-gather.9.cloned.1.call-start = ((), (), s32[]{:S(2)}) async-start(), calls=%async_computation.5 | async-start | bytes 3538944 | tf_op jit(solution)/shard_map/all_gather | solution.py:128
  133.4 10.8 %all-to-all-start.2 = ((s32[8,1,8]{2,1,0:T(1,128)}), s32[8,1,8]{2,1,0:T(1,128)S(1)}, u32[]{:S(2)}, u32[]{:S(2)}) async-start(s32[8,1,8]{2,1,0:T(1,128)} %bitcast.6), calls=%async_computation.2 | async-start | bytes 8192 | tf_op jit(solution)/shard_map/all_to_all | solution.py:91
  137.8 778.8 %all-gather.17.cloned.1.call-start = ((), (), s32[]{:S(2)}) async-start(), calls=%async_computation.9 | async-start | bytes 2162688 | tf_op jit(solution)/shard_map/all_gather | solution.py:101
  154.4 155.7 %copy-start.1 = (s32[1536]{0:T(1024)S(1)}, s32[1536]{0:T(1024)}, u32[]{:S(2)}) copy-start(s32[1536]{0:T(1024)} %param.19) | copy-start | bytes 18436
  310.1 606.5 %copy-start.10 = (s32[64]{0:T(128)S(1)}, s32[64]{0:T(128)}, u32[]{:S(2)}) copy-start(s32[64]{0:T(128)} %copy-done.9) | copy-start | bytes 772
  457.8 1.2 copy-start.2
  608.3 1.2 copy-start.2
  759.9 1.2 copy-start.2
  911.5 1.2 copy-start.2
  916.5 12.7 %copy-start.12 = (s32[64]{0:T(128)S(1)}, s32[64]{0:T(128)}, u32[]{:S(2)}) copy-start(s32[64]{0:T(128)} %copy-done.11) | copy-start | bytes 772
  (2 other events, 1.3 us)
Sparse Core Ops, SparseCore 0:
  11.0 59.7 all-gather.12
  73.8 55.3 all-gather.6
  132.2 55.3 all-gather.10
  189.6 59.2 all-gather.14
  251.0 59.0 all-gather.8
  312.9 55.1 all-gather.16
where the time goes:
time: 938 us; the launch traced here: 937 us
  local copies, waits for them, and re-layouts  566 us (60%)
  waiting for transfers between devices  259 us (28%)
  matrix products  51.5 us (5%)
  blocking collectives  19.1 us (2%)
  between operations  15.7 us (2%)
  starting transfers between devices  15.3 us (2%)
  other arithmetic  9.68 us (1%)
    gather x8, local copies, waits for them, and re-layouts, absorb(): jnp.take(bucket_table, jnp.clip(distance, 0, bucket_table.shape[0] - 1),...  542 us
    all_gather x1, waiting for transfers between devices, shards(): part_keys = lax.all_gather(keys_here, 'tok', axis=0, tiled=True)  61.1 us
    all_gather x1, waiting for transfers between devices, shards(): part_values = lax.all_gather(values_here, 'tok', axis=0, tiled=True)  58.3 us
    all_gather x1, waiting for transfers between devices, shards(): lax.all_gather(w_key, ('fsdp', 'tok'), axis=0, tiled=True)  54.8 us
    all_gather x1, waiting for transfers between devices, shards(): lax.all_gather(w_query, ('fsdp', 'tok'), axis=0, tiled=True)  33.1 us
    all_gather x1, waiting for transfers between devices, shards(): lax.all_gather(w_value, ('fsdp', 'tok'), axis=0, tiled=True)  32.8 us
  transfers between devices with their start and end apart: 9, of which 8 were waited for; matrix products, arithmetic and copies ran while one was open for 66% of the time, Pallas kernels for 0%

commit v1 on v0

--- a/solution.py
+++ b/solution.py
@@ -5,6 +5,27 @@
 
 far_away = 1073741824
 neg_floor = -1e30
+
+
+def laid_out(blocks, dim):
+    blocks = jnp.moveaxis(blocks, 0, dim)
+    shape = blocks.shape
+    return blocks.reshape(*shape[:dim], shape[dim] * shape[dim + 1], *shape[dim + 2 :])
+
+
+def collected_by_bits(value, axis):
+    size, here = (lax.axis_size(axis), lax.axis_index(axis))
+    blocks, distance = (value[None], 1)
+    while distance < size:
+        theirs = lax.ppermute(blocks, axis, [(i, i ^ distance) for i in range(size)])
+        low = here & distance == 0
+        blocks = jnp.concatenate([jnp.where(low, blocks, theirs), jnp.where(low, theirs, blocks)])
+        distance *= 2
+    return blocks
+
+
+def doubled_up(x, axis, dim):
+    return laid_out(collected_by_bits(x, axis), dim)
 
 
 def bias_scores(bucket_ids, bias_parts):
@@ -95,7 +116,7 @@
     dealt = permute_rows(place_sel, got_rows.reshape(tok_rows, feature_count))
     dealt_pos = permute_ints(place_sel, got_pos.reshape(tok_rows))
     query_w, key_w, value_w, out_w = (
-        lax.all_gather(w_query, ("fsdp", "tok"), axis=0, tiled=True),
+        doubled_up(w_query, ("fsdp", "tok"), 0),
         lax.all_gather(w_key, ("fsdp", "tok"), axis=0, tiled=True),
         lax.all_gather(w_value, ("fsdp", "tok"), axis=0, tiled=True),
         lax.all_gather(w_out, ("fsdp", "tok"), axis=0, tiled=True),

time: 938 us -> 890 us (0.949)
  waiting for transfers between devices: 259 us -> 209 us
    all_gather x1, waiting for transfers between devices: 58.3 us -> 5.13 us  [shards(): part_values = lax.all_gather(values_here, 'tok', axis=0, tiled=True)]
    ppermute x0 -> x5, waiting for transfers between devices: none -> 35.6 us  [collected_by_bits(): lax.ppermute(blocks, axis, [(i, i ^ distance) for i in range(size)])]
    all_gather x1 -> x0, waiting for transfers between devices: 33.1 us -> none  [shards(): lax.all_gather(w_query, ('fsdp', 'tok'), axis=0, tiled=True)]
  transfers between devices with their start and end apart: 9 -> 13, of which waited for: 8 -> 12; matrix products, arithmetic and copies ran while one was open for 66% -> 70% of each run, Pallas kernels for 0% -> 0%
where the time goes in v1:
time: 890 us; the launch traced here: 889 us
  local copies, waits for them, and re-layouts  566 us (64%)
  waiting for transfers between devices  209 us (23%)
  matrix products  50.1 us (6%)
  blocking collectives  19.2 us (2%)
  starting transfers between devices  18.3 us (2%)
  between operations  15.4 us (2%)
  other arithmetic  11.4 us (1%)
    gather x8, local copies, waits for them, and re-layouts, absorb(): jnp.take(bucket_table, jnp.clip(distance, 0, bucket_table.shape[0] - 1),...  542 us
    all_gather x1, waiting for transfers between devices, shards(): part_keys = lax.all_gather(keys_here, 'tok', axis=0, tiled=True)  61.1 us
    all_gather x1, waiting for transfers between devices, shards(): lax.all_gather(w_key, ('fsdp', 'tok'), axis=0, tiled=True)  54.8 us
    ppermute x5, waiting for transfers between devices, collected_by_bits(): lax.ppermute(blocks, axis, [(i, i ^ distance) for i in range(size)])  35.6 us
    all_gather x1, waiting for transfers between devices, shards(): lax.all_gather(w_value, ('fsdp', 'tok'), axis=0, tiled=True)  33.2 us
  transfers between devices with their start and end apart: 13, of which 12 were waited for; matrix products, arithmetic and copies ran while one was open for 70% of the time, Pallas kernels for 0%

profile of v1, /device:TPU:0, one launch (start us, length us, event | category | flops | bytes accessed | tf_op | source)
XLA Modules:
  0.0 889.4 jit_solution(1824857813488719651)
XLA Ops:
  11.0 7.3 all-to-all-start
  19.2 5.6 all-to-all-done
  24.7 3.4 all-to-all-start.1
  28.3 7.3 all-to-all-done.1
  37.3 33.2 %all-gather.10.cloned.1.call-done = bf16[1024,1024]{1,0:T(8,128)(2,1)} async-done(((bf16[32,1024]{1,0:T(8,128)(2,1)}), bf16[1024,1024]{1,0:T(8,128)(2,1)}) %all-gather.10.cloned.1.call-update) | async-done | bytes 2097168 | tf_op jit(solution)/shard_map/all_gather | solution.py:121
  74.1 54.8 %all-gather.6.cloned.1.call-done = bf16[1024,1024]{1,0:T(8,128)(2,1)} async-done(((bf16[32,1024]{1,0:T(8,128)(2,1)}), bf16[1024,1024]{1,0:T(8,128)(2,1)}) %all-gather.6.cloned.1.call-update) | async-done | bytes 2097168 | tf_op jit(solution)/shard_map/all_gather | solution.py:120
  134.0 2.8 collective-permute-done
  137.5 7.9 collective-permute-done.1
  145.5 20.3 %collective-permute-done.2 = bf16[4,32,1024]{2,1,0:T(8,128)(2,1)S(1)} collective-permute-done((bf16[4,32,1024]{2,1,0:T(8,128)(2,1)S(1)}, bf16[4,32,1024]{2,1,0:T(8,128)(2,1)S(1)}, u32[]{:S(2)}, u32[]{:S(2)}) %collective-permute-start.2) | collective-permute-done | bytes 262176 | tf_op jit(solution)/shard_map/ppermute | solution.py:20
  171.3 3.6 all-to-all-start.2
  177.5 3.9 all-to-all-done.2
  183.0 8.8 all-reduce
  196.4 5.1 all-gather.12.cloned.1.call-done
  201.5 61.1 %all-gather.8.cloned.1.call-done = bf16[1536,1024]{1,0:T(8,128)(2,1)} async-done(((bf16[192,1024]{1,0:T(8,128)(2,1)}), bf16[1536,1024]{1,0:T(8,128)(2,1)}) %all-gather.8.cloned.1.call-update) | async-done | bytes 3145744 | tf_op jit(solution)/shard_map/all_gather | solution.py:149
  262.7 605.5 %while.15 = (s32[]{:T(128)}, f32[64,16,64]{0,2,1:T(8,128)}, f32[16,64]{1,0:T(8,128)S(1)}, f32[16,64]{1,0:T(8,128)S(1)}, s32[64]{0:T(128)S(1)}, /*index=5*/s32[4,...) while((s32[]{:T(128)}, f32[64,16,64]{0,2,1:T(8,128)}, ...), condition=%wide.region_8.9_spmd.clone, body=%wide.region_5.8_spmd.clone.sunk | while | flops 183465984 | bytes 27471288 | solution.py:176
  262.8 135.5 %gather_fusion = s32[24576]{0:T(1024)S(1)} fusion(s32[1536]{0:T(1024)S(1)} %get-tuple-element.345, s32[24576]{0:T(1024)S(1)} %broadcast_clamp_fusion.2), kind=kCustom, calls=%fused_computation.clone.clone.1 | custom fusion | bytes 294912 | tf_op jit(solution)/shard_map/while/body/eval_jaxpr/jit(_take)/gather | solution.py:52
  406.3 4.1 select_reduce_fusion.5
  413.4 135.5 %gather_fusion = s32[24576]{0:T(1024)S(1)} fusion(s32[1536]{0:T(1024)S(1)} %get-tuple-element.345, s32[24576]{0:T(1024)S(1)} %broadcast_clamp_fusion.2), kind=kCustom, calls=%fused_computation.clone.clone.1 | custom fusion | bytes 294912 | tf_op jit(solution)/shard_map/while/body/eval_jaxpr/jit(_take)/gather | solution.py:52
  556.9 4.1 select_reduce_fusion.5
  565.1 135.5 %gather_fusion = s32[24576]{0:T(1024)S(1)} fusion(s32[1536]{0:T(1024)S(1)} %get-tuple-element.345, s32[24576]{0:T(1024)S(1)} %broadcast_clamp_fusion.2), kind=kCustom, calls=%fused_computation.clone.clone.1 | custom fusion | bytes 294912 | tf_op jit(solution)/shard_map/while/body/eval_jaxpr/jit(_take)/gather | solution.py:52
  708.6 4.1 select_reduce_fusion.5
  716.7 135.5 %gather_fusion = s32[24576]{0:T(1024)S(1)} fusion(s32[1536]{0:T(1024)S(1)} %get-tuple-element.345, s32[24576]{0:T(1024)S(1)} %broadcast_clamp_fusion.2), kind=kCustom, calls=%fused_computation.clone.clone.1 | custom fusion | bytes 294912 | tf_op jit(solution)/shard_map/while/body/eval_jaxpr/jit(_take)/gather | solution.py:52
  860.2 4.1 select_reduce_fusion.5
  871.6 10.4 %all_to_all.25 = bf16[8,8,1024]{2,1,0:T(8,128)(2,1)S(1)} all-to-all(bf16[8,8,1024]{2,1,0:T(8,128)(2,1)S(1)} %fusion.25), channel_id=1, replica_groups=mesh['fsdp'=4,'tok'=8] {'tok'}, dimensions={0} | all-to-all | bytes 262144 | tf_op jit(solution)/shard_map/all_to_all | solution.py:189
  (171 shorter events, 79.6 us)
Async XLA Ops:
  7.2 11.2 %copy-start = (bf16[1,64,1024]{2,1,0:T(8,128)(2,1)S(1)}, bf16[1,64,1024]{2,1,0:T(8,128)(2,1)}, u32[]{:S(2)}) copy-start(bf16[1,64,1024]{2,1,0:T(8,128)(2,1)} %param.14) | copy-start | bytes 393220
  7.2 63.3 %all-gather.10.cloned.1.call-start = ((), (), s32[]{:S(2)}) async-start(), calls=%async_computation.6 | async-start | bytes 2162688 | tf_op jit(solution)/shard_map/all_gather | solution.py:121
  7.9 121.0 %all-gather.6.cloned.1.call-start = ((), (), s32[]{:S(2)}) async-start(), calls=%async_computation.4 | async-start | bytes 2162688 | tf_op jit(solution)/shard_map/all_gather | solution.py:120
  9.6 15.1 %copy-start.12 = (s32[64]{0:T(128)}, s32[64]{0:T(128)S(1)}, u32[]{:S(2)}) copy-start(s32[64]{0:T(128)S(1)} %convert_reduce_fusion) | copy-start | bytes 772
  11.0 13.7 %all-to-all-start = ((s32[8,1,8]{2,1,0:T(1,128)}), s32[8,1,8]{2,1,0:T(1,128)S(1)}, u32[]{:S(2)}, u32[]{:S(2)}) async-start(s32[8,1,8]{2,1,0:T(1,128)} %bitcast.1), calls=%async_computation | async-start | bytes 8192 | tf_op jit(solution)/shard_map/all_to_all | solution.py:111
  24.7 10.8 %all-to-all-start.1 = ((bf16[8,8,1024]{2,1,0:T(8,128)(2,1)}), bf16[8,8,1024]{2,1,0:T(8,128)(2,1)S(1)}, u32[]{:S(2)}, u32[]{:S(2)}) async-start(bf16[8,8,1024]{2,1,0:T(8,128)(2,1)} %fusion.26), calls=%async_computation.1 | async-start | bytes 262144 | tf_op jit(solution)/shard_map/all_to_all | solution.py:110
  28.1 173.4 %all-gather.12.cloned.1.call-start = ((), (), s32[]{:S(2)}) async-start(), calls=%async_computation.7 | async-start | bytes 3538944 | tf_op jit(solution)/shard_map/all_gather | solution.py:150
  28.3 154.5 %copy-start.10 = (s32[64]{0:T(128)}, s32[64]{0:T(128)S(1)}, u32[]{:S(2)}) copy-start(s32[64]{0:T(128)S(1)} %sub.69) | copy-start | bytes 772
  28.3 45.0 %copy-start.6 = (bf16[1,128,1024]{2,1,0:T(8,128)(2,1)S(1)}, bf16[1,128,1024]{2,1,0:T(8,128)(2,1)}, u32[]{:S(2)}) copy-start(bf16[1,128,1024]{2,1,0:T(8,128)(2,1)} %param.16) | copy-start | bytes 786436
  74.1 57.6 %copy-start.7 = (bf16[1,128,1024]{2,1,0:T(8,128)(2,1)S(1)}, bf16[1,128,1024]{2,1,0:T(8,128)(2,1)}, u32[]{:S(2)}) copy-start(bf16[1,128,1024]{2,1,0:T(8,128)(2,1)} %param.15) | copy-start | bytes 786436
  74.1 58.4 %copy-start.8 = (bf16[32,1024]{1,0:T(8,128)(2,1)S(1)}, bf16[32,1024]{1,0:T(8,128)(2,1)}, u32[]{:S(2)}) copy-start(bf16[32,1024]{1,0:T(8,128)(2,1)} %param.22) | copy-start | bytes 196612
  74.1 188.6 %all-gather.8.cloned.1.call-start = ((), (), s32[]{:S(2)}) async-start(), calls=%async_computation.5 | async-start | bytes 3538944 | tf_op jit(solution)/shard_map/all_gather | solution.py:149
  132.4 4.3 collective-permute-start
  136.8 8.5 collective-permute-start.1
  145.4 20.4 %collective-permute-start.2 = (bf16[4,32,1024]{2,1,0:T(8,128)(2,1)S(1)}, bf16[4,32,1024]{2,1,0:T(8,128)(2,1)S(1)}, u32[]{:S(2)}, u32[]{:S(2)}) collective-permute-start(bf16[4,32,1024]{2,1,0:T(8,128)(2,1)S(1)} %pad_maximum_fusion.5), channel_id=1, source_target_pairs={{0,4},{1,5},{2,6},{3,7},{4,0},{5,1},{6,2},{7,3},{8,12},{9,13},{10,... | collective-permute-start | bytes 786440 | tf_op jit(solution)/shard_map/ppermute | solution.py:20
  165.9 2.0 collective-permute-start.3
  168.0 8.2 copy-start.9
  168.0 8.3 copy-start.14
  169.2 25.4 %collective-permute-start.4 = (bf16[16,32,1024]{2,1,0:T(8,128)(2,1)}, bf16[16,32,1024]{2,1,0:T(8,128)(2,1)S(1)}, u32[]{:S(2)}, u32[]{:S(2)}) collective-permute-start(bf16[16,32,1024]{2,1,0:T(8,128)(2,1)} %pad_maximum_fusion.1), channel_id=1, source_target_pairs={{0,16},{1,17},{2,18},{3,19},{4,20},{5,21},{6,22},{7,23},{8,24},{9,... | collective-permute-start | bytes 3145736 | tf_op jit(solution)/shard_map/ppermute | solution.py:20
  171.3 10.2 %all-to-all-start.2 = ((s32[8,1,8]{2,1,0:T(1,128)}), s32[8,1,8]{2,1,0:T(1,128)S(1)}, u32[]{:S(2)}, u32[]{:S(2)}) async-start(s32[8,1,8]{2,1,0:T(1,128)} %bitcast.6), calls=%async_computation.2 | async-start | bytes 8192 | tf_op jit(solution)/shard_map/all_to_all | solution.py:112
  174.9 694.4 %all-gather.14.cloned.1.call-start = ((), (), s32[]{:S(2)}) async-start(), calls=%async_computation.8 | async-start | bytes 2162688 | tf_op jit(solution)/shard_map/all_gather | solution.py:122
  194.9 67.7 %copy-start.1 = (s32[1536]{0:T(1024)S(1)}, s32[1536]{0:T(1024)}, u32[]{:S(2)}) copy-start(s32[1536]{0:T(1024)} %param.19) | copy-start | bytes 18436
  262.7 606.7 %copy-start.11 = (s32[64]{0:T(128)S(1)}, s32[64]{0:T(128)}, u32[]{:S(2)}) copy-start(s32[64]{0:T(128)} %copy-done.10) | copy-start | bytes 772
  869.3 12.7 %copy-start.13 = (s32[64]{0:T(128)S(1)}, s32[64]{0:T(128)}, u32[]{:S(2)}) copy-start(s32[64]{0:T(128)} %copy-done.12) | copy-start | bytes 772
  (7 other events, 6.7 us)
Sparse Core Ops, SparseCore 0:
  11.0 59.4 all-gather.9
  73.5 55.3 all-gather.5
  131.1 70.3 all-gather.11
  203.6 59.0 all-gather.7
  265.5 55.1 all-gather.13
